TPU v7x, 32 devices: a whole 2x2x4 slice. The times are simulated.
32 devices in a mesh: section: 2 (over core), expert: 8 (over z, x), dp: 2 (over y).
Axes of the slice: x: 2, y: 2, z: 4, core: 2. Of those that a mesh axis runs over, the one named last changes fastest.
Arguments:
- tokens: bfloat16 [2, 16, 65, 768], P(None, ('expert', 'dp')), may hold values from -6 to 6
- cotangent: bfloat16 [2, 16, 65, 768], P(None, ('expert', 'dp')), may hold values from -6 to 6
- routes: int32 [2, 2, 16, 65, 2], P('section', None, ('expert', 'dp')), may hold values from 0 to 7, all different within a row; in each aligned block of 65 rows (0 to 64, 65 to 129, ..., all dimensions but the last counted through in order) at most 25 rows name the same one
- norm1_gain: bfloat16 [2, 768], P('section', 'dp'), may hold values from 0.099609375 to 1.8984375
- qkv_weight: bfloat16 [2, 768, 2304], P('section', 'dp'), may hold values from -1 to 1
- out_weight: bfloat16 [2, 768, 768], P('section', 'dp'), may hold values from -1.25 to 1.25
- norm2_gain: bfloat16 [2, 768], P('section', 'dp'), may hold values from 0.099609375 to 1.8984375
- router_weight: bfloat16 [2, 768, 8], P('section', 'dp'), may hold values from -1 to 1
- expert_in: bfloat16 [2, 8, 768, 3072], P('section', 'expert', None, 'dp'), may hold values from -0.21875 to 0.21875
- expert_out: bfloat16 [2, 8, 3072, 768], P('section', 'expert', 'dp'), may hold values from -0.875 to 0.875
Outputs:
- boundary: float32 [2, 2, 16, 65, 768], P('section', None, ('expert', 'dp'))
- grad_norm1: float32 [2, 768], P('section', 'dp')
- grad_qkv: float32 [2, 768, 2304], P('section', 'dp')
- grad_proj: float32 [2, 768, 768], P('section', 'dp')
- grad_norm2: float32 [2, 768], P('section', 'dp')
- grad_router: float32 [2, 768, 8], P('section', 'dp')
- grad_expert_in: float32 [2, 8, 768, 3072], P('section', 'expert', None, 'dp')
- grad_expert_out: float32 [2, 8, 3072, 768], P('section', 'expert', 'dp')
Inputs may be any that keep to these rules, and one draw needn't show every extreme that they name: `routes`: in every aligned block of 65 rows (the images of one device in one micro-batch of one section) no expert is named by more than 25 rows, a bound that some block reaches; the two experts of a token differ.
All inputs are finite; a program needn't handle non-finite values.
Results may differ from a plain program's by a relative error of at most 0.03.
Values may be sent and summed in bfloat16 or wider, within the bound.
No kernel may reach another device: no remote copies, remote signals or barrier semaphores. Data moves between devices by JAX's collectives and lax.ppermute only.
A program may use at most 192 MiB of HBM per device.

v0:
```python
import jax
import jax.numpy as jnp
from jax import lax
from jax.sharding import PartitionSpec as P

HEAD = 64
EPSILON = 1e-06


def passed_along(value, axis, steps):
    count = lax.axis_size(axis)
    leading, last = (max(0, -steps), min(count, count - steps))
    return lax.ppermute(value, axis, [(source, source + steps) for source in range(leading, last)])


def shortened(x):
    return jax.tree.map(lambda a: a.astype(jnp.bfloat16) if a.dtype == jnp.float32 else a, x)


def norm_forward(values, norm_gain):
    center = values - jnp.mean(values, axis=-1, keepdims=True)
    inverse = lax.rsqrt(jnp.mean(center * center, axis=-1, keepdims=True) + EPSILON)
    normed = center * inverse
    return (normed * norm_gain, normed, inverse)


def norm_backward(grad_out, normed, inverse, norm_gain):
    grad_hat = grad_out * norm_gain
    grad_gain = jnp.sum(grad_out * normed, axis=0)
    grad_in = inverse * (
        grad_hat
        - jnp.mean(grad_hat, axis=-1, keepdims=True)
        - normed * jnp.mean(grad_hat * normed, axis=-1, keepdims=True)
    )
    return (grad_in, grad_gain)


def gelu_slope(pre_act):
    return (
        0.5 * (1.0 + lax.erf(pre_act * 0.7071067811865476))
        + pre_act * jnp.exp(-0.5 * pre_act * pre_act) * 0.3989422804014327
    )


def attention_forward(a_norm, weight_qkv, images):
    heads = weight_qkv.shape[1] // (3 * HEAD)
    qkv_rows = jnp.dot(a_norm, weight_qkv, preferred_element_type=jnp.float32).astype(jnp.bfloat16)
    shaped = qkv_rows.reshape(images, -1, 3, heads, HEAD)
    scores = jnp.einsum(
        "ishd,ithd->ihst", shaped[:, :, 0], shaped[:, :, 1], preferred_element_type=jnp.float32
    ) * HEAD ** (-0.5)
    row_max = jnp.max(scores, axis=-1, keepdims=True)
    log_total = row_max + jnp.log(jnp.sum(jnp.exp(scores - row_max), axis=-1, keepdims=True))
    attn_probs = jnp.exp(scores - log_total).astype(jnp.bfloat16)
    attended = jnp.einsum(
        "ihst,ithd->ishd", attn_probs, shaped[:, :, 2], preferred_element_type=jnp.float32
    )
    attended = attended.astype(jnp.bfloat16).reshape(a_norm.shape[0], heads * HEAD)
    return (qkv_rows, log_total, attended)


def attention_backward(grad_attended, qkv_rows, log_total, images):
    heads = qkv_rows.shape[1] // (3 * HEAD)
    shaped = qkv_rows.reshape(images, -1, 3, heads, HEAD)
    query_part = shaped[:, :, 0]
    key_part = shaped[:, :, 1]
    value_part = shaped[:, :, 2]
    score_scale = HEAD ** (-0.5)
    scores = (
        jnp.einsum("ishd,ithd->ihst", query_part, key_part, preferred_element_type=jnp.float32)
        * score_scale
    )
    attn_probs = jnp.exp(scores - log_total)
    probs_low = attn_probs.astype(jnp.bfloat16)
    grad_heads = grad_attended.reshape(images, -1, heads, HEAD)
    grad_value = jnp.einsum(
        "ihst,ishd->ithd", probs_low, grad_heads, preferred_element_type=jnp.float32
    )
    grad_probs = jnp.einsum(
        "ishd,ithd->ihst", grad_heads, value_part, preferred_element_type=jnp.float32
    )
    grad_scores = (
        attn_probs
        * (grad_probs - jnp.sum(attn_probs * grad_probs, axis=-1, keepdims=True))
        * score_scale
    )
    grad_scores = grad_scores.astype(jnp.bfloat16)
    grad_query = jnp.einsum(
        "ihst,ithd->ishd", grad_scores, key_part, preferred_element_type=jnp.float32
    )
    grad_key = jnp.einsum(
        "ihst,ishd->ithd", grad_scores, query_part, preferred_element_type=jnp.float32
    )
    stacked = jnp.stack([grad_query, grad_key, grad_value], axis=2)
    return stacked.astype(jnp.bfloat16).reshape(qkv_rows.shape[0], 3 * heads * HEAD)


def shards(
    tokens,
    cotangent,
    routes,
    norm1_gain,
    qkv_weight,
    out_weight,
    norm2_gain,
    router_weight,
    expert_in,
    expert_out,
):
    gathered = (
        lax.all_gather(norm1_gain, "dp", axis=1, tiled=True),
        lax.all_gather(qkv_weight, "dp", axis=1, tiled=True),
        lax.all_gather(out_weight, "dp", axis=1, tiled=True),
        lax.all_gather(norm2_gain, "dp", axis=1, tiled=True),
        lax.all_gather(router_weight, "dp", axis=1, tiled=True),
    )
    norm_one, weight_qkv, weight_proj, norm_two, weight_router = [member[0] for member in gathered]
    gain_one = norm_one.astype(jnp.float32)
    gain_two = norm_two.astype(jnp.float32)
    weight_in = expert_in[0, 0]
    weight_back = expert_out[0, 0]
    section_id = lax.axis_index("section")
    micro_count = tokens.shape[0]
    images = tokens.shape[1]
    seq_len = tokens.shape[2]
    model_width = tokens.shape[3]
    token_count = images * seq_len
    experts = weight_router.shape[1]
    capacity = max(2, (3 * token_count + experts - 1) // experts)
    pair_size = lax.axis_size("dp")
    section_routes = routes[0]

    def owner_trip(send_rows, work):
        spread = jnp.broadcast_to(
            send_rows.reshape(experts, 1, capacity, model_width),
            (experts, pair_size, capacity, model_width),
        )
        spread = spread.reshape(experts * pair_size, capacity, model_width)
        group_rows = lax.all_to_all(
            spread, ("expert", "dp"), split_axis=0, concat_axis=0, tiled=True
        )
        result, extra_out = work(group_rows)
        returned = lax.all_to_all(
            result.astype(jnp.bfloat16), ("expert", "dp"), split_axis=0, concat_axis=0, tiled=True
        ).astype(result.dtype)
        slot_total = jnp.sum(returned.reshape(experts, pair_size, capacity, model_width), axis=1)
        slot_total = slot_total.reshape(experts * capacity, model_width)
        return (slot_total, group_rows, extra_out)

    def expert_forward_work(group_rows):
        pre_act = jnp.einsum(
            "ksd,df->ksf", group_rows, weight_in, preferred_element_type=jnp.float32
        )
        hidden = jax.nn.gelu(pre_act, approximate=False).astype(jnp.bfloat16)
        return (
            jnp.einsum("ksf,fd->ksd", hidden, weight_back, preferred_element_type=jnp.float32),
            None,
        )

    def layer_backward(grad_in, kept_state):
        (
            a_norm,
            hat_one,
            inv_one,
            qkv_rows,
            log_total,
            attended,
            hat_two,
            inv_two,
            b_norm,
            router,
            pair_ids,
            gate_vals,
            slot_place,
            dispatch,
            group_rows,
            expert_rows,
        ) = kept_state
        grad_gate = jnp.sum(grad_in[:, None, :] * expert_rows.astype(jnp.float32), axis=-1)
        grad_rows = (
            (gate_vals[:, :, None] * grad_in[:, None, :])
            .astype(jnp.bfloat16)
            .reshape(-1, model_width)
        )
        send_grads = jnp.dot(dispatch, grad_rows, preferred_element_type=jnp.float32).astype(
            jnp.bfloat16
        )

        def expert_backward_work(group_grads):
            pre_act = jnp.einsum(
                "ksd,df->ksf", group_rows, weight_in, preferred_element_type=jnp.float32
            )
            hidden = jax.nn.gelu(pre_act, approximate=False).astype(jnp.bfloat16)
            grad_weight_back = jnp.einsum(
                "ksf,ksd->fd", hidden, group_grads, preferred_element_type=jnp.float32
            )
            grad_hidden = jnp.einsum(
                "ksd,fd->ksf", group_grads, weight_back, preferred_element_type=jnp.float32
            )
            grad_pre = (grad_hidden * gelu_slope(pre_act)).astype(jnp.bfloat16)
            grad_weight_in = jnp.einsum(
                "ksd,ksf->df", group_rows, grad_pre, preferred_element_type=jnp.float32
            )
            grad_slot_rows = jnp.einsum(
                "ksf,df->ksd", grad_pre, weight_in, preferred_element_type=jnp.float32
            )
            return (grad_slot_rows, (grad_weight_in, grad_weight_back))

        grad_total, unused, expert_terms = owner_trip(send_grads, expert_backward_work)
        grad_b_expert = jnp.sum(
            jnp.take(grad_total, slot_place, axis=0).reshape(token_count, 2, model_width), axis=1
        )
        choose = (
            pair_ids[:, :, None] == jnp.arange(experts, dtype=jnp.int32)[None, None, :]
        ).astype(jnp.float32)
        grad_prob = jnp.sum(choose * grad_gate[:, :, None], axis=1)
        grad_logit = router * (grad_prob - jnp.sum(router * grad_prob, axis=-1, keepdims=True))
        grad_logit = grad_logit.astype(jnp.bfloat16)
        grad_router_w = jnp.dot(b_norm.T, grad_logit, preferred_element_type=jnp.float32)
        grad_b = (
            jnp.dot(grad_logit, weight_router.T, preferred_element_type=jnp.float32) + grad_b_expert
        )
        grad_resid_norm, grad_gain_two = norm_backward(grad_b, hat_two, inv_two, gain_two)
        grad_resid = grad_in + grad_resid_norm
        grad_low = grad_resid.astype(jnp.bfloat16)
        grad_proj_w = jnp.dot(attended.T, grad_low, preferred_element_type=jnp.float32)
        grad_attended = jnp.dot(grad_low, weight_proj.T, preferred_element_type=jnp.float32).astype(
            jnp.bfloat16
        )
        grad_qkv_rows = attention_backward(grad_attended, qkv_rows, log_total, images)
        grad_qkv_w = jnp.dot(a_norm.T, grad_qkv_rows, preferred_element_type=jnp.float32)
        grad_a = jnp.dot(grad_qkv_rows, weight_qkv.T, preferred_element_type=jnp.float32)
        grad_token_norm, grad_gain_one = norm_backward(grad_a, hat_one, inv_one, gain_one)
        grad_tokens = grad_resid + grad_token_norm
        dense_terms = (grad_gain_one, grad_qkv_w, grad_proj_w, grad_gain_two, grad_router_w)
        return (grad_tokens, dense_terms, expert_terms)

    zero_rows = jnp.zeros((images, seq_len, model_width), jnp.bfloat16)
    forward_state = []
    forward_out = []
    passed = zero_rows
    for tick_index in range(micro_count + 1):
        if tick_index > 0:
            passed = passed_along(section_output, "section", 1)
        layer_in = jnp.where(section_id == 0, tokens[min(tick_index, micro_count - 1)], passed)
        micro_id = jnp.clip(tick_index - section_id, 0, micro_count - 1)
        route_ids = lax.dynamic_index_in_dim(section_routes, micro_id, 0, keepdims=False)
        token_rows = layer_in.reshape(token_count, model_width).astype(jnp.float32)
        a_full, layer_hat_one, layer_inv_one = norm_forward(token_rows, gain_one)
        layer_a_norm = a_full.astype(jnp.bfloat16)
        layer_qkv_rows, layer_log_total, layer_attended = attention_forward(
            layer_a_norm, weight_qkv, images
        )
        residual = token_rows + jnp.dot(
            layer_attended, weight_proj, preferred_element_type=jnp.float32
        )
        b_full, layer_hat_two, layer_inv_two = norm_forward(residual, gain_two)
        layer_b_norm = b_full.astype(jnp.bfloat16)
        logits = jnp.dot(layer_b_norm, weight_router, preferred_element_type=jnp.float32)
        layer_router = jax.nn.softmax(logits, axis=-1)
        layer_pair_ids = route_ids.reshape(token_count, 2)
        layer_gate_vals = jnp.take_along_axis(layer_router, layer_pair_ids, axis=1)
        flat_routes = route_ids.reshape(-1)
        onehot = (flat_routes[:, None] == jnp.arange(experts, dtype=jnp.int32)[None, :]).astype(
            jnp.int32
        )
        slot_pos = jnp.sum(onehot * (jnp.cumsum(onehot, axis=0) - 1), axis=1)
        slot_slot_place = flat_routes * capacity + slot_pos
        slot_dispatch = (
            slot_slot_place[None, :] == jnp.arange(experts * capacity, dtype=jnp.int32)[:, None]
        ).astype(jnp.bfloat16)
        layer_send_rows = jnp.dot(
            slot_dispatch, jnp.repeat(layer_b_norm, 2, axis=0), preferred_element_type=jnp.float32
        ).astype(jnp.bfloat16)
        layer_slot_total, layer_group_rows, layer_unused = owner_trip(
            layer_send_rows, expert_forward_work
        )
        slot_out = layer_slot_total.astype(jnp.bfloat16)
        layer_expert_rows = jnp.take(slot_out, slot_slot_place, axis=0).reshape(
            token_count, 2, model_width
        )
        layer_out = residual + jnp.sum(
            layer_gate_vals[:, :, None] * layer_expert_rows.astype(jnp.float32), axis=1
        )
        layer_kept_state = (
            layer_a_norm,
            layer_hat_one,
            layer_inv_one,
            layer_qkv_rows,
            layer_log_total,
            layer_attended,
            layer_hat_two,
            layer_inv_two,
            layer_b_norm,
            layer_router,
            layer_pair_ids,
            layer_gate_vals,
            slot_slot_place,
            slot_dispatch,
            layer_group_rows,
            layer_expert_rows,
        )
        layer_out, kept_state = (layer_out, layer_kept_state)
        section_output = layer_out.astype(jnp.bfloat16).reshape(images, seq_len, model_width)
        forward_state.append(kept_state)
        forward_out.append(layer_out)
    dense_sum = None
    expert_sum = None
    grad_inputs = []
    grad_carry = zero_rows
    for tick_index in range(micro_count + 1):
        kept_state = forward_state[micro_count - tick_index]
        own_cot = cotangent[micro_count - 1 - tick_index] if tick_index < micro_count else zero_rows
        passed_grad = passed_along(grad_carry, "section", -1) if tick_index > 0 else zero_rows
        grad_in = (
            jnp.where(section_id == 1, own_cot, passed_grad)
            .reshape(token_count, model_width)
            .astype(jnp.float32)
        )
        grad_tokens, dense_terms, expert_terms = layer_backward(grad_in, kept_state)
        grad_carry = grad_tokens.astype(jnp.bfloat16).reshape(images, seq_len, model_width)
        grad_inputs.append(grad_tokens)
        if dense_sum is None:
            dense_sum = dense_terms
            expert_sum = expert_terms
        else:
            dense_sum = tuple(
                (
                    first_term + second_term
                    for first_term, second_term in zip(dense_sum, dense_terms)
                )
            )
            expert_sum = tuple(
                (
                    first_term + second_term
                    for first_term, second_term in zip(expert_sum, expert_terms)
                )
            )
    end_values = []
    for micro_index in range(micro_count):
        picked = jnp.where(
            section_id == 0, grad_inputs[micro_count - micro_index], forward_out[micro_index + 1]
        )
        end_values.append(picked.reshape(images, seq_len, model_width))
    boundary = jnp.stack(end_values)[None]
    shares = jax.tree.map(
        lambda part: part.astype(jnp.float32),
        lax.psum_scatter(shortened(dense_sum), "dp", scatter_dimension=0, tiled=True),
    )
    full_sums = jax.tree.map(
        lambda part: part.astype(jnp.float32), lax.psum(shortened(shares), "expert")
    )
    return (
        boundary,
        full_sums[0][None],
        full_sums[1][None],
        full_sums[2][None],
        full_sums[3][None],
        full_sums[4][None],
        expert_sum[0][None, None],
        expert_sum[1][None, None],
    )


def solution(mesh):
    in_specs = (
        P(None, ("expert", "dp"), None, None),
        P(None, ("expert", "dp"), None, None),
        P("section", None, ("expert", "dp"), None, None),
        P("section", "dp"),
        P("section", "dp", None),
        P("section", "dp", None),
        P("section", "dp"),
        P("section", "dp", None),
        P("section", "expert", None, "dp"),
        P("section", "expert", "dp", None),
    )
    out_specs = (
        P("section", None, ("expert", "dp"), None, None),
        P("section", "dp"),
        P("section", "dp", None),
        P("section", "dp", None),
        P("section", "dp"),
        P("section", "dp", None),
        P("section", "expert", None, "dp"),
        P("section", "expert", "dp", None),
    )
    return jax.shard_map(shards, mesh=mesh, in_specs=in_specs, out_specs=out_specs, check_vma=False)
```

profile of v0, /device:TPU:0, one launch (start us, length us, event | category | flops | bytes accessed | tf_op | source)
XLA Modules:
  0.0 877.7 jit_solution(11960009164507809311)
XLA Ops:
  8.7 5.5 all_gather.15
  14.2 4.5 all_gather.18
  23.4 38.3 %all-gather.3.cloned.1.call-done = bf16[1,768,2304]{2,1,0:T(8,128)(2,1)} async-done(((bf16[1,384,2304]{2,1,0:T(8,128)(2,1)}), bf16[1,768,2304]{2,1,0:T(8,128)(2,1)}) %all-gather.3.cloned.1.call-update) | async-done | bytes 3538960 | tf_op jit(solution)/shard_map/all_gather | solution.py:112
  68.2 17.7 %all-gather.5.cloned.1.call-done = bf16[1,768,768]{2,1,0:T(8,128)(2,1)} async-done(((bf16[1,384,768]{2,1,0:T(8,128)(2,1)}), bf16[1,768,768]{2,1,0:T(8,128)(2,1)}) %all-gather.5.cloned.1.call-update) | async-done | bytes 1179664 | tf_op jit(solution)/shard_map/all_gather | solution.py:113
  93.1 5.7 all-to-all-start
  101.4 17.0 %all-to-all-done = bf16[16,25,768]{2,1,0:T(8,128)(2,1)} async-done(((bf16[16,25,768]{2,1,0:T(8,128)(2,1)}), bf16[16,25,768]{2,1,0:T(8,128)(2,1)}, u32[]{:S(2)}, u32[]{:S(2)}) %all-to-all-start) | async-done | bytes 614432 | tf_op jit(solution)/shard_map/all_to_all | solution.py:139
  123.2 7.0 fusion.28
  133.6 5.0 all-to-all-start.1
  139.0 4.9 all_gather.19
  147.9 9.4 %all-to-all-done.1 = bf16[16,25,768]{2,1,0:T(8,128)(2,1)} async-done(((bf16[16,25,768]{2,1,0:T(8,128)(2,1)}), bf16[16,25,768]{2,1,0:T(8,128)(2,1)}, u32[]{:S(2)}, u32[]{:S(2)}) %all-to-all-start.1) | async-done | bytes 614432 | tf_op jit(solution)/shard_map/all_to_all | solution.py:143
  188.9 26.6 %all_to_all.60 = bf16[16,25,768]{2,1,0:T(8,128)(2,1)S(1)} all-to-all(bf16[16,25,768]{2,1,0:T(8,128)(2,1)S(1)} %bitcast.575), channel_id=1, replica_groups=mesh['section'=2,'expert'=8,'dp'=2] {'expert','dp'}, dimensions={0} | all-to-all | bytes 1228800 | tf_op jit(solution)/shard_map/all_to_all | solution.py:139
  219.1 7.0 fusion.31
  243.1 9.4 %all-to-all-done.3 = bf16[16,25,768]{2,1,0:T(8,128)(2,1)} async-done(((bf16[16,25,768]{2,1,0:T(8,128)(2,1)}), bf16[16,25,768]{2,1,0:T(8,128)(2,1)}, u32[]{:S(2)}, u32[]{:S(2)}) %all-to-all-start.3) | async-done | bytes 614432 | tf_op jit(solution)/shard_map/all_to_all | solution.py:143
  290.1 26.6 %all_to_all.61 = bf16[16,25,768]{2,1,0:T(8,128)(2,1)S(1)} all-to-all(bf16[16,25,768]{2,1,0:T(8,128)(2,1)S(1)} %bitcast.576), channel_id=1, replica_groups=mesh['section'=2,'expert'=8,'dp'=2] {'expert','dp'}, dimensions={0} | all-to-all | bytes 1228800 | tf_op jit(solution)/shard_map/all_to_all | solution.py:139
  320.3 7.0 fusion.34
  330.7 4.5 all-to-all-start.5
  345.3 8.5 all-to-all-done.5
  377.6 24.9 %all_to_all.62 = bf16[16,25,768]{2,1,0:T(8,128)(2,1)S(1)} all-to-all(bf16[16,25,768]{2,1,0:T(8,128)(2,1)S(1)} %bitcast.577), channel_id=1, replica_groups=mesh['section'=2,'expert'=8,'dp'=2] {'expert','dp'}, dimensions={0} | all-to-all | bytes 1228800 | tf_op jit(solution)/shard_map/all_to_all | solution.py:139
  415.3 17.8 %all-to-all-done.7 = bf16[16,25,768]{2,1,0:T(8,128)(2,1)} async-done(((bf16[16,25,768]{2,1,0:T(8,128)(2,1)}), bf16[16,25,768]{2,1,0:T(8,128)(2,1)}, u32[]{:S(2)}, u32[]{:S(2)}) %all-to-all-start.7) | async-done | bytes 614432 | tf_op jit(solution)/shard_map/all_to_all | solution.py:143
  481.5 26.4 %all_to_all.63 = bf16[16,25,768]{2,1,0:T(8,128)(2,1)S(1)} all-to-all(bf16[16,25,768]{2,1,0:T(8,128)(2,1)S(1)} %bitcast.578), channel_id=1, replica_groups=mesh['section'=2,'expert'=8,'dp'=2] {'expert','dp'}, dimensions={0} | all-to-all | bytes 1228800 | tf_op jit(solution)/shard_map/all_to_all | solution.py:139
  513.8 23.9 %all_to_all.64 = bf16[16,25,768]{2,1,0:T(8,128)(2,1)S(1)} all-to-all(bf16[16,25,768]{2,1,0:T(8,128)(2,1)S(1)} %fusion.98), channel_id=1, replica_groups=mesh['section'=2,'expert'=8,'dp'=2] {'expert','dp'}, dimensions={0} | all-to-all | bytes 1228800 | tf_op jit(solution)/shard_map/all_to_all | solution.py:143
  590.5 24.2 %all_to_all.65 = bf16[16,25,768]{2,1,0:T(8,128)(2,1)S(1)} all-to-all(bf16[16,25,768]{2,1,0:T(8,128)(2,1)S(1)} %bitcast.579), channel_id=1, replica_groups=mesh['section'=2,'expert'=8,'dp'=2] {'expert','dp'}, dimensions={0} | all-to-all | bytes 1228800 | tf_op jit(solution)/shard_map/all_to_all | solution.py:139
  631.3 14.0 %all-to-all-done.11 = bf16[16,25,768]{2,1,0:T(8,128)(2,1)S(1)} async-done(((bf16[16,25,768]{2,1,0:T(8,128)(2,1)}), bf16[16,25,768]{2,1,0:T(8,128)(2,1)S(1)}, u32[]{:S(2)}, u32[]{:S(2)}) %all-to-all-start.11) | async-done | bytes 614432 | tf_op jit(solution)/shard_map/all_to_all | solution.py:143
  666.9 5.3 fusion.320
  678.6 8.3 add_convert_fusion
  689.9 5.2 fusion.337
  708.0 8.2 fusion.4
  716.3 22.3 %reduce-scatter.6.cloned.1.call-done = bf16[384,2304]{1,0:T(8,128)(2,1)} async-done(((bf16[768,2304]{1,0:T(8,128)(2,1)}), bf16[384,2304]{1,0:T(8,128)(2,1)}) %reduce-scatter.6.cloned.1.call-update) | async-done | bytes 1769488 | tf_op jit(solution)/shard_map/reduce_scatter | solution.py:348
  738.7 8.2 fusion.3
  749.5 4.9 all-reduce.7
  760.3 23.4 %all-reduce.5 = (bf16[1,384]{1,0:T(2,128)(2,1)S(1)}, bf16[1,384]{1,0:T(2,128)(2,1)S(1)}, bf16[1,384,8]{1,2,0:T(8,128)(2,1)S(1)}) all-reduce(bf16[1,384]{1,0:T(2,128)(2,1)S(1)} %broadcast_in_dim.104, bf16[1,384]{1,0:T(2,128)(2,1)S(1)} %broadcast_in_dim.110, ...), channel_id=1, replica_groups=mesh['section'=2,'expert'=8,'dp'=2] {'expert'}, use_global_device_ids=true, to_apply=%region_73.77 | all-reduce | flops 3840 | bytes 15360 | tf_op jit(solution)/shard_map/psum | solution.py:351
  785.4 79.4 %all-reduce.10.cloned.1.call-done = (bf16[1,384,2304]{2,1,0:T(8,128)(2,1)}, bf16[1,384,768]{2,1,0:T(8,128)(2,1)}) async-done(((bf16[1,384,2304]{2,1,0:T(8,128)(2,1)}, bf16[1,384,768]{2,1,0:T(8,128)(2,1)}), (bf16[1,384,2304]{2,1,0:T(8,128)(2,1)}, bf16[1,384,768]{2,1,0:T(8,128)(2,1)})) %all-reduce.10.cloned.1.call-update) | async-done | bytes 2359312 | tf_op jit(solution)/shard_map/psum | solution.py:351
  (604 shorter events, 359.8 us)
Async XLA Ops:
  7.2 111.2 %copy-start = (bf16[1,1,768,1536]{3,2,1,0:T(8,128)(2,1)S(1)}, bf16[1,1,768,1536]{3,2,1,0:T(8,128)(2,1)}, u32[]{:S(2)}) copy-start(bf16[1,1,768,1536]{3,2,1,0:T(8,128)(2,1)} %param.24) | copy-start | bytes 7077892
  7.2 54.5 %all-gather.3.cloned.1.call-start = ((), (), s32[]{:S(2)}) async-start(), calls=%async_computation.15 | async-start | bytes 5308416 | tf_op jit(solution)/shard_map/all_gather | solution.py:112
  7.9 78.0 %all-gather.5.cloned.1.call-start = ((), (), s32[]{:S(2)}) async-start(), calls=%async_computation.16 | async-start | bytes 1769472 | tf_op jit(solution)/shard_map/all_gather | solution.py:113
  20.0 45.5 %copy-start.100 = (s32[1,1,1,65,2]{3,4,2,1,0:T(2,128)}, s32[1,1,1,65,2]{3,4,2,1,0:T(2,128)S(1)}, u32[]{:S(2)}) copy-start(s32[1,1,1,65,2]{3,4,2,1,0:T(2,128)S(1)} %get-tuple-element.81) | copy-start | bytes 1564
  20.0 79.6 %copy-start.99 = (s32[1,1,1,65,2]{3,4,2,1,0:T(2,128)}, s32[1,1,1,65,2]{3,4,2,1,0:T(2,128)S(1)}, u32[]{:S(2)}) copy-start(s32[1,1,1,65,2]{3,4,2,1,0:T(2,128)S(1)} %get-tuple-element.105) | copy-start | bytes 1564
  20.0 127.1 %copy-start.98 = (s32[1,1,1,65,2]{3,4,2,1,0:T(2,128)}, s32[1,1,1,65,2]{3,4,2,1,0:T(2,128)S(1)}, u32[]{:S(2)}) copy-start(s32[1,1,1,65,2]{3,4,2,1,0:T(2,128)S(1)} %get-tuple-element.103) | copy-start | bytes 1564
  21.5 79.9 %copy-start.95 = (s32[130]{0:T(256)}, s32[130]{0:T(256)S(1)}, u32[]{:S(2)}) copy-start(s32[130]{0:T(256)S(1)} %get-tuple-element.95) | copy-start | bytes 1564
  21.6 139.9 %copy-start.129 = (pred[130]{0:T(512)(128)(4,1)}, pred[130]{0:T(512)(128)(4,1)S(1)}, u32[]{:S(2)}) copy-start(pred[130]{0:T(512)(128)(4,1)S(1)} %get-tuple-element.94) | copy-start | bytes 394
  23.0 145.2 %copy-start.40 = (bf16[1,1,65,768]{3,0,2,1:T(2,128)(2,1)}, bf16[1,1,65,768]{3,0,2,1:T(2,128)(2,1)S(1)}, u32[]{:S(2)}) copy-start(bf16[1,1,65,768]{3,0,2,1:T(2,128)(2,1)S(1)} %get-tuple-element.100) | copy-start | bytes 299524
  23.1 62.9 %copy-start.18 = (bf16[1,1,65,768]{3,2,1,0:T(8,128)(2,1)}, bf16[1,1,65,768]{3,2,1,0:T(8,128)(2,1)S(1)}, u32[]{:S(2)}) copy-start(bf16[1,1,65,768]{3,2,1,0:T(8,128)(2,1)S(1)} %get-tuple-element.97) | copy-start | bytes 299524
  23.1 43.9 %copy-start.104 = (f32[65]{0:T(128)}, f32[65]{0:T(128)S(1)}, u32[]{:S(2)}) copy-start(f32[65]{0:T(128)S(1)} %broadcast_multiply_fusion.17) | copy-start | bytes 784
  23.3 44.9 %copy-start.121 = (f32[65]{0:T(128)}, f32[65]{0:T(128)S(1)}, u32[]{:S(2)}) copy-start(f32[65]{0:T(128)S(1)} %add_rsqrt_fusion.5) | copy-start | bytes 784
  23.4 156.2 %copy-start.68 = (f32[768]{0:T(1024)}, f32[768]{0:T(1024)S(1)}, u32[]{:S(2)}) copy-start(f32[768]{0:T(1024)S(1)} %convert_reduce_fusion.6) | copy-start | bytes 9220
  67.0 26.1 %copy-start.76 = (f32[12,65]{1,0:T(8,128)}, f32[12,65]{1,0:T(8,128)S(1)}, u32[]{:S(2)}) copy-start(f32[12,65]{1,0:T(8,128)S(1)} %log_add_fusion.2) | copy-start | bytes 9364
  87.7 78.1 %copy-start.8 = (f32[65,768]{1,0:T(8,128)}, f32[65,768]{1,0:T(8,128)S(1)}, u32[]{:S(2)}) copy-start(f32[65,768]{1,0:T(8,128)S(1)} %get-tuple-element.113) | copy-start | bytes 599044
  88.1 56.4 %copy-start.43 = (bf16[65,768]{1,0:T(8,128)(2,1)}, bf16[65,768]{1,0:T(8,128)(2,1)S(1)}, u32[]{:S(2)}) copy-start(bf16[65,768]{1,0:T(8,128)(2,1)S(1)} %multiply_convert_fusion.5) | copy-start | bytes 299524
  93.1 25.3 %all-to-all-start = ((bf16[16,25,768]{2,1,0:T(8,128)(2,1)}), bf16[16,25,768]{2,1,0:T(8,128)(2,1)}, u32[]{:S(2)}, u32[]{:S(2)}) async-start(bf16[16,25,768]{2,1,0:T(8,128)(2,1)} %bitcast.574), calls=%async_computation | async-start | bytes 1572864 | tf_op jit(solution)/shard_map/all_to_all | solution.py:139
  133.6 23.7 %all-to-all-start.1 = ((bf16[16,25,768]{2,1,0:T(8,128)(2,1)}), bf16[16,25,768]{2,1,0:T(8,128)(2,1)}, u32[]{:S(2)}, u32[]{:S(2)}) async-start(bf16[16,25,768]{2,1,0:T(8,128)(2,1)} %fusion.104), calls=%async_computation.1 | async-start | bytes 1572864 | tf_op jit(solution)/shard_map/all_to_all | solution.py:143
  165.9 2.2 collective-permute-start
  167.8 67.8 %copy-start.96 = (s32[130]{0:T(256)}, s32[130]{0:T(256)S(1)}, u32[]{:S(2)}) copy-start(s32[130]{0:T(256)S(1)} %get-tuple-element.138) | copy-start | bytes 1564
  229.5 23.0 %all-to-all-start.3 = ((bf16[16,25,768]{2,1,0:T(8,128)(2,1)}), bf16[16,25,768]{2,1,0:T(8,128)(2,1)}, u32[]{:S(2)}, u32[]{:S(2)}) async-start(bf16[16,25,768]{2,1,0:T(8,128)(2,1)} %fusion.107), calls=%async_computation.3 | async-start | bytes 1572864 | tf_op jit(solution)/shard_map/all_to_all | solution.py:143
  266.3 2.2 collective-permute-start.1
  280.6 38.0 %copy-start.117 = (f32[65]{0:T(128)}, f32[65]{0:T(128)S(1)}, u32[]{:S(2)}) copy-start(f32[65]{0:T(128)S(1)} %broadcast_multiply_fusion.12) | copy-start | bytes 784
  330.7 23.0 %all-to-all-start.5 = ((bf16[16,25,768]{2,1,0:T(8,128)(2,1)}), bf16[16,25,768]{2,1,0:T(8,128)(2,1)}, u32[]{:S(2)}, u32[]{:S(2)}) async-start(bf16[16,25,768]{2,1,0:T(8,128)(2,1)} %fusion.110), calls=%async_computation.5 | async-start | bytes 1572864 | tf_op jit(solution)/shard_map/all_to_all | solution.py:143
  410.4 22.7 %all-to-all-start.7 = ((bf16[16,25,768]{2,1,0:T(8,128)(2,1)}), bf16[16,25,768]{2,1,0:T(8,128)(2,1)}, u32[]{:S(2)}, u32[]{:S(2)}) async-start(bf16[16,25,768]{2,1,0:T(8,128)(2,1)} %fusion.95), calls=%async_computation.7 | async-start | bytes 1572864 | tf_op jit(solution)/shard_map/all_to_all | solution.py:143
  468.4 3.5 collective-permute-start.2
  578.2 3.5 collective-permute-start.3
  622.6 22.7 %all-to-all-start.11 = ((bf16[16,25,768]{2,1,0:T(8,128)(2,1)}), bf16[16,25,768]{2,1,0:T(8,128)(2,1)S(1)}, u32[]{:S(2)}, u32[]{:S(2)}) async-start(bf16[16,25,768]{2,1,0:T(8,128)(2,1)} %fusion.101), calls=%async_computation.11 | async-start | bytes 1572864 | tf_op jit(solution)/shard_map/all_to_all | solution.py:143
  626.3 89.9 %reduce-scatter.8.cloned.1.call-start = ((), (), s32[]{:S(2)}) async-start(), calls=%async_computation.18 | async-start | bytes 1769472 | tf_op jit(solution)/shard_map/reduce_scatter | solution.py:348
  666.8 71.8 %reduce-scatter.6.cloned.1.call-start = ((), (), s32[]{:S(2)}) async-start(), calls=%async_computation.17 | async-start | bytes 5308416 | tf_op jit(solution)/shard_map/reduce_scatter | solution.py:348
  687.0 72.3 %reduce-scatter.10.cloned.1.call-start = ((), (), s32[]{:S(2)}) async-start(), calls=%async_computation.19 | async-start | bytes 294912
  708.0 156.9 %all-reduce.10.cloned.1.call-start = ((), (), s32[]{:S(2)}) async-start(), calls=%async_computation.20 | async-start | bytes 4718592 | tf_op jit(solution)/shard_map/psum | solution.py:351
  (128 other events, 672.2 us)
Sparse Core Ops, SparseCore 0:
  9.5 52.0 all-gather.2
  63.2 22.7 all-gather.4
  666.9 21.1 reduce-scatter.7
  690.8 47.7 reduce-scatter.5
  740.6 11.0 reduce-scatter.9
  755.1 109.6 all-reduce.9
where the time goes:
time: 890 us; the launch traced here: 878 us
  waiting for transfers between devices  239 us (27%)
  blocking collectives  196 us (22%)
  matrix products  166 us (19%)
  local copies, waits for them, and re-layouts  131 us (15%)
  other arithmetic  95.5 us (11%)
  starting transfers between devices  33.4 us (4%)
  between operations  17 us (2%)
    all_to_all x5, blocking collectives, owner_trip(): lax.all_to_all(spread, ('expert', 'dp'), split_axis=0, concat_axis=0, til...  129 us
    psum x1, waiting for transfers between devices, shards(): lax.psum(shortened(shares), 'expert')  79.4 us
    all_to_all x5, waiting for transfers between devices, owner_trip(): lax.all_to_all(result.astype(jnp.bfloat16), ('expert', 'dp'), split_axis=...  59 us
    all_gather x1, waiting for transfers between devices, shards(): lax.all_gather(qkv_weight, 'dp', axis=1, tiled=True)  38.3 us
    unnamed x294, local copies, waits for them, and re-layouts  26.3 us
    all_to_all x1, blocking collectives, owner_trip(): lax.all_to_all(result.astype(jnp.bfloat16), ('expert', 'dp'), split_axis=...  23.9 us
    psum x1, blocking collectives, shards(): lax.psum(shortened(shares), 'expert')  23.4 us
    reduce_scatter x2, waiting for transfers between devices, shards(): lax.psum_scatter(shortened(dense_sum), 'dp', scatter_dimension=0, tiled=T...  22.3 us
  transfers between devices with their start and end apart: 16, of which 14 were waited for; matrix products, arithmetic and copies ran while one was open for 12% of the time, Pallas kernels for 0%

commit v1 on v0

--- a/solution.py
+++ b/solution.py
@@ -5,6 +5,29 @@
 
 HEAD = 64
 EPSILON = 1e-06
+
+
+def split_up(x, dim, size):
+    before, after = (x.shape[:dim], x.shape[dim + 1 :])
+    return jnp.moveaxis(x.reshape(*before, size, -1, *after), dim, 0)
+
+
+def in_order(tiles, dim):
+    shape = list(tiles.shape[1:])
+    shape[dim] *= tiles.shape[0]
+    return jnp.moveaxis(tiles, 0, dim).reshape(shape)
+
+
+def rotated_exchange(value, axis, split_dim, concat_dim):
+    size, here = (lax.axis_size(axis), lax.axis_index(axis))
+    blocks = split_up(value, split_dim, size)
+    out = blocks
+    for turn in range(1, size):
+        target, source = ((here + turn) % size, (here - turn) % size)
+        sent = lax.dynamic_index_in_dim(blocks, target, 0)
+        other = lax.ppermute(sent, axis, [(i, (i + turn) % size) for i in range(size)])
+        out = lax.dynamic_update_slice_in_dim(out, other, source, axis=0)
+    return in_order(out, concat_dim)
 
 
 def passed_along(value, axis, steps):
@@ -136,9 +159,7 @@
             (experts, pair_size, capacity, model_width),
         )
         spread = spread.reshape(experts * pair_size, capacity, model_width)
-        group_rows = lax.all_to_all(
-            spread, ("expert", "dp"), split_axis=0, concat_axis=0, tiled=True
-        )
+        group_rows = rotated_exchange(spread, ("expert", "dp"), 0, 0)
         result, extra_out = work(group_rows)
         returned = lax.all_to_all(
             result.astype(jnp.bfloat16), ("expert", "dp"), split_axis=0, concat_axis=0, tiled=True

time: 890 us -> 1130 us (1.27)
  waiting for transfers between devices: 239 us -> 467 us
  starting transfers between devices: 33.4 us -> 174 us
  blocking collectives: 196 us -> 64.9 us
    ppermute x0 -> x90, waiting for transfers between devices: none -> 272 us  [rotated_exchange(): lax.ppermute(sent, axis, [(i, (i + turn) % size) for i in range(size)])]
    ppermute x0 -> x90, starting transfers between devices: none -> 135 us  [rotated_exchange(): lax.ppermute(sent, axis, [(i, (i + turn) % size) for i in range(size)])]
    all_to_all x5 -> x0, blocking collectives: 129 us -> none  [owner_trip(): lax.all_to_all(spread, ('expert', 'dp'), split_axis=0, concat_axis=0, til...]
    all_to_all x5, waiting for transfers between devices: 59 us -> 30.8 us  [owner_trip(): lax.all_to_all(result.astype(jnp.bfloat16), ('expert', 'dp'), split_axis=...]
    all_to_all x1 -> x0, waiting for transfers between devices: 17 us -> none  [owner_trip(): lax.all_to_all(spread, ('expert', 'dp'), split_axis=0, concat_axis=0, til...]
    all_to_all x5, starting transfers between devices: 22 us -> 33.6 us  [owner_trip(): lax.all_to_all(result.astype(jnp.bfloat16), ('expert', 'dp'), split_axis=...]
    unnamed x294 -> x316, local copies, waits for them, and re-layouts: 26.3 us -> 26.9 us
  transfers between devices with their start and end apart: 16 -> 105, of which waited for: 14 -> 74; matrix products, arithmetic and copies ran while one was open for 12% -> 10% of each run, Pallas kernels for 0% -> 0%
where the time goes in v1:
time: 1130 us; the launch traced here: 1120 us
  waiting for transfers between devices  467 us (41%)
  starting transfers between devices  174 us (15%)
  matrix products  162 us (14%)
  local copies, waits for them, and re-layouts  141 us (12%)
  other arithmetic  94 us (8%)
  blocking collectives  64.9 us (6%)
  between operations  18.3 us (2%)
    ppermute x90, waiting for transfers between devices, rotated_exchange(): lax.ppermute(sent, axis, [(i, (i + turn) % size) for i in range(size)])  272 us
    ppermute x90, starting transfers between devices, rotated_exchange(): lax.ppermute(sent, axis, [(i, (i + turn) % size) for i in range(size)])  135 us
    psum x1, waiting for transfers between devices, shards(): lax.psum(shortened(shares), 'expert')  83.6 us
    all_gather x1, waiting for transfers between devices, shards(): lax.all_gather(qkv_weight, 'dp', axis=1, tiled=True)  35.6 us
    all_to_all x5, starting transfers between devices, owner_trip(): lax.all_to_all(result.astype(jnp.bfloat16), ('expert', 'dp'), split_axis=...  33.6 us
    all_to_all x5, waiting for transfers between devices, owner_trip(): lax.all_to_all(result.astype(jnp.bfloat16), ('expert', 'dp'), split_axis=...  30.8 us
    unnamed x316, local copies, waits for them, and re-layouts  26.9 us
    psum x1, blocking collectives, shards(): lax.psum(shortened(shares), 'expert')  23.5 us
  transfers between devices with their start and end apart: 105, of which 74 were waited for; matrix products, arithmetic and copies ran while one was open for 10% of the time, Pallas kernels for 0%

profile of v1, /device:TPU:0, one launch (start us, length us, event | category | flops | bytes accessed | tf_op | source)
XLA Modules:
  0.0 1121.7 jit_solution(14150184074577540299)
XLA Ops:
  26.1 35.6 %all-gather.3.cloned.1.call-done = bf16[1,768,2304]{2,1,0:T(8,128)(2,1)} async-done(((bf16[1,384,2304]{2,1,0:T(8,128)(2,1)}), bf16[1,768,2304]{2,1,0:T(8,128)(2,1)}) %all-gather.3.cloned.1.call-update) | async-done | bytes 3538960 | tf_op jit(solution)/shard_map/all_gather | solution.py:135
  67.9 18.1 %all-gather.5.cloned.1.call-done = bf16[1,768,768]{2,1,0:T(8,128)(2,1)} async-done(((bf16[1,384,768]{2,1,0:T(8,128)(2,1)}), bf16[1,768,768]{2,1,0:T(8,128)(2,1)}) %all-gather.5.cloned.1.call-update) | async-done | bytes 1179664 | tf_op jit(solution)/shard_map/all_gather | solution.py:136
  173.0 7.0 fusion.28
  183.4 7.0 all-to-all-start
  243.2 6.5 collective-permute-done.17
  249.6 6.8 collective-permute-done.18
  307.0 7.0 fusion.31
  317.4 7.0 all-to-all-start.1
  383.0 6.5 collective-permute-done.33
  389.5 6.8 collective-permute-done.34
  447.7 7.0 fusion.34
  458.1 6.7 all-to-all-start.2
  510.3 6.5 collective-permute-done.48
  516.8 7.0 collective-permute-done.49
  529.9 6.5 collective-permute-done.51
  578.5 6.6 all-to-all-start.3
  585.8 12.3 %all-to-all-done.3 = bf16[16,25,768]{2,1,0:T(8,128)(2,1)} async-done(((bf16[16,25,768]{2,1,0:T(8,128)(2,1)}), bf16[16,25,768]{2,1,0:T(8,128)(2,1)}, u32[]{:S(2)}, u32[]{:S(2)}) %all-to-all-start.3) | async-done | bytes 614432 | tf_op jit(solution)/shard_map/all_to_all | solution.py:164
  655.2 6.6 collective-permute-done.64
  661.8 6.8 collective-permute-done.65
  674.7 6.5 collective-permute-done.67
  720.4 21.6 %all_to_all.30 = bf16[16,25,768]{2,1,0:T(8,128)(2,1)S(1)} all-to-all(bf16[16,25,768]{2,1,0:T(8,128)(2,1)S(1)} %fusion.98), channel_id=1, replica_groups=mesh['section'=2,'expert'=8,'dp'=2] {'expert','dp'}, dimensions={0} | all-to-all | bytes 1228800 | tf_op jit(solution)/shard_map/all_to_all | solution.py:164
  803.0 6.8 collective-permute-done.80
  809.8 6.8 collective-permute-done.81
  822.5 7.1 collective-permute-done.83
  829.7 6.5 collective-permute-done.84
  881.7 8.1 all-to-all-done.5
  923.1 8.1 add_convert_fusion
  951.7 8.1 fusion.4
  959.9 23.1 %reduce-scatter.6.cloned.1.call-done = bf16[384,2304]{1,0:T(8,128)(2,1)} async-done(((bf16[768,2304]{1,0:T(8,128)(2,1)}), bf16[384,2304]{1,0:T(8,128)(2,1)}) %reduce-scatter.6.cloned.1.call-update) | async-done | bytes 1769488 | tf_op jit(solution)/shard_map/reduce_scatter | solution.py:369
  983.0 8.0 fusion.3
  999.9 23.5 %all-reduce.5 = (bf16[1,384]{1,0:T(2,128)(2,1)S(1)}, bf16[1,384]{1,0:T(2,128)(2,1)S(1)}, bf16[1,384,8]{1,2,0:T(8,128)(2,1)S(1)}) all-reduce(bf16[1,384]{1,0:T(2,128)(2,1)S(1)} %broadcast_in_dim.104, bf16[1,384]{1,0:T(2,128)(2,1)S(1)} %broadcast_in_dim.110, ...), channel_id=1, replica_groups=mesh['section'=2,'expert'=8,'dp'=2] {'expert'}, use_global_device_ids=true, to_apply=%region_73.77 | all-reduce | flops 3840 | bytes 15360 | tf_op jit(solution)/shard_map/psum | solution.py:372
  1025.2 83.6 %all-reduce.10.cloned.1.call-done = (bf16[1,384,2304]{2,1,0:T(8,128)(2,1)}, bf16[1,384,768]{2,1,0:T(8,128)(2,1)}) async-done(((bf16[1,384,2304]{2,1,0:T(8,128)(2,1)}, bf16[1,384,768]{2,1,0:T(8,128)(2,1)}), (bf16[1,384,2304]{2,1,0:T(8,128)(2,1)}, bf16[1,384,768]{2,1,0:T(8,128)(2,1)})) %all-reduce.10.cloned.1.call-update) | async-done | bytes 2359312 | tf_op jit(solution)/shard_map/psum | solution.py:372
  (895 shorter events, 711.5 us)
Async XLA Ops:
  7.2 54.5 %all-gather.3.cloned.1.call-start = ((), (), s32[]{:S(2)}) async-start(), calls=%async_computation.9 | async-start | bytes 5308416 | tf_op jit(solution)/shard_map/all_gather | solution.py:135
  7.9 78.1 %all-gather.5.cloned.1.call-start = ((), (), s32[]{:S(2)}) async-start(), calls=%async_computation.10 | async-start | bytes 1769472 | tf_op jit(solution)/shard_map/all_gather | solution.py:136
  94.9 72.7 %collective-permute-start.14 = (bf16[1,1,25,768]{3,2,1,0:T(8,128)(2,1)S(1)}, bf16[1,1,25,768]{3,2,1,0:T(8,128)(2,1)S(1)}, u32[]{:S(2)}, u32[]{:S(2)}) collective-permute-start(bf16[1,1,25,768]{3,2,1,0:T(8,128)(2,1)S(1)} %get-tuple-element.173), channel_id=1, source_target_pairs={{0,15},{1,0},{2,1},{3,2},{4,3},{5,4},{6,5},{7,6},{8,7},{9,8},{10,9... | collective-permute-start | bytes 115208 | tf_op jit(solution)/shard_map/ppermute | solution.py:28
  100.2 66.7 %collective-permute-start.13 = (bf16[1,1,25,768]{3,2,1,0:T(8,128)(2,1)S(1)}, bf16[1,1,25,768]{3,2,1,0:T(8,128)(2,1)S(1)}, u32[]{:S(2)}, u32[]{:S(2)}) collective-permute-start(bf16[1,1,25,768]{3,2,1,0:T(8,128)(2,1)S(1)} %get-tuple-element.174), channel_id=1, source_target_pairs={{0,14},{1,15},{2,0},{3,1},{4,2},{5,3},{6,4},{7,5},{8,6},{9,7},{10,... | collective-permute-start | bytes 115208 | tf_op jit(solution)/shard_map/ppermute | solution.py:28
  101.8 64.6 %collective-permute-start.12 = (bf16[1,1,25,768]{3,2,1,0:T(8,128)(2,1)S(1)}, bf16[1,1,25,768]{3,2,1,0:T(8,128)(2,1)S(1)}, u32[]{:S(2)}, u32[]{:S(2)}) collective-permute-start(bf16[1,1,25,768]{3,2,1,0:T(8,128)(2,1)S(1)} %get-tuple-element.175), channel_id=1, source_target_pairs={{0,13},{1,14},{2,15},{3,0},{4,1},{5,2},{6,3},{7,4},{8,5},{9,6},{10... | collective-permute-start | bytes 115208 | tf_op jit(solution)/shard_map/ppermute | solution.py:28
  101.8 63.9 %collective-permute-start.11 = (bf16[1,1,25,768]{3,2,1,0:T(8,128)(2,1)S(1)}, bf16[1,1,25,768]{3,2,1,0:T(8,128)(2,1)S(1)}, u32[]{:S(2)}, u32[]{:S(2)}) collective-permute-start(bf16[1,1,25,768]{3,2,1,0:T(8,128)(2,1)S(1)} %get-tuple-element.176), channel_id=1, source_target_pairs={{0,12},{1,13},{2,14},{3,15},{4,0},{5,1},{6,2},{7,3},{8,4},{9,5},{1... | collective-permute-start | bytes 115208 | tf_op jit(solution)/shard_map/ppermute | solution.py:28
  183.4 20.0 %all-to-all-start = ((bf16[16,25,768]{2,1,0:T(8,128)(2,1)}), bf16[16,25,768]{2,1,0:T(8,128)(2,1)}, u32[]{:S(2)}, u32[]{:S(2)}) async-start(bf16[16,25,768]{2,1,0:T(8,128)(2,1)} %fusion.104), calls=%async_computation | async-start | bytes 1572864 | tf_op jit(solution)/shard_map/all_to_all | solution.py:164
  236.3 66.9 %collective-permute-start.30 = (bf16[1,1,25,768]{3,2,1,0:T(8,128)(2,1)S(1)}, bf16[1,1,25,768]{3,2,1,0:T(8,128)(2,1)S(1)}, u32[]{:S(2)}, u32[]{:S(2)}) collective-permute-start(bf16[1,1,25,768]{3,2,1,0:T(8,128)(2,1)S(1)} %get-tuple-element.158), channel_id=1, source_target_pairs={{0,15},{1,0},{2,1},{3,2},{4,3},{5,4},{6,5},{7,6},{8,7},{9,8},{10,9... | collective-permute-start | bytes 115208 | tf_op jit(solution)/shard_map/ppermute | solution.py:28
  240.5 62.7 %collective-permute-start.29 = (bf16[1,1,25,768]{3,2,1,0:T(8,128)(2,1)S(1)}, bf16[1,1,25,768]{3,2,1,0:T(8,128)(2,1)S(1)}, u32[]{:S(2)}, u32[]{:S(2)}) collective-permute-start(bf16[1,1,25,768]{3,2,1,0:T(8,128)(2,1)S(1)} %get-tuple-element.159), channel_id=1, source_target_pairs={{0,14},{1,15},{2,0},{3,1},{4,2},{5,3},{6,4},{7,5},{8,6},{9,7},{10,... | collective-permute-start | bytes 115208 | tf_op jit(solution)/shard_map/ppermute | solution.py:28
  241.2 62.0 %collective-permute-start.28 = (bf16[1,1,25,768]{3,2,1,0:T(8,128)(2,1)S(1)}, bf16[1,1,25,768]{3,2,1,0:T(8,128)(2,1)S(1)}, u32[]{:S(2)}, u32[]{:S(2)}) collective-permute-start(bf16[1,1,25,768]{3,2,1,0:T(8,128)(2,1)S(1)} %get-tuple-element.160), channel_id=1, source_target_pairs={{0,13},{1,14},{2,15},{3,0},{4,1},{5,2},{6,3},{7,4},{8,5},{9,6},{10... | collective-permute-start | bytes 115208 | tf_op jit(solution)/shard_map/ppermute | solution.py:28
  241.2 62.0 %collective-permute-start.27 = (bf16[1,1,25,768]{3,2,1,0:T(8,128)(2,1)S(1)}, bf16[1,1,25,768]{3,2,1,0:T(8,128)(2,1)S(1)}, u32[]{:S(2)}, u32[]{:S(2)}) collective-permute-start(bf16[1,1,25,768]{3,2,1,0:T(8,128)(2,1)S(1)} %get-tuple-element.161), channel_id=1, source_target_pairs={{0,12},{1,13},{2,14},{3,15},{4,0},{5,1},{6,2},{7,3},{8,4},{9,5},{1... | collective-permute-start | bytes 115208 | tf_op jit(solution)/shard_map/ppermute | solution.py:28
  317.4 20.0 %all-to-all-start.1 = ((bf16[16,25,768]{2,1,0:T(8,128)(2,1)}), bf16[16,25,768]{2,1,0:T(8,128)(2,1)}, u32[]{:S(2)}, u32[]{:S(2)}) async-start(bf16[16,25,768]{2,1,0:T(8,128)(2,1)} %fusion.107), calls=%async_computation.1 | async-start | bytes 1572864 | tf_op jit(solution)/shard_map/all_to_all | solution.py:164
  376.2 67.8 %collective-permute-start.46 = (bf16[1,1,25,768]{3,2,1,0:T(8,128)(2,1)S(1)}, bf16[1,1,25,768]{3,2,1,0:T(8,128)(2,1)S(1)}, u32[]{:S(2)}, u32[]{:S(2)}) collective-permute-start(bf16[1,1,25,768]{3,2,1,0:T(8,128)(2,1)S(1)} %get-tuple-element.143), channel_id=1, source_target_pairs={{0,15},{1,0},{2,1},{3,2},{4,3},{5,4},{6,5},{7,6},{8,7},{9,8},{10,9... | collective-permute-start | bytes 115208 | tf_op jit(solution)/shard_map/ppermute | solution.py:28
  380.4 63.6 %collective-permute-start.45 = (bf16[1,1,25,768]{3,2,1,0:T(8,128)(2,1)S(1)}, bf16[1,1,25,768]{3,2,1,0:T(8,128)(2,1)S(1)}, u32[]{:S(2)}, u32[]{:S(2)}) collective-permute-start(bf16[1,1,25,768]{3,2,1,0:T(8,128)(2,1)S(1)} %get-tuple-element.144), channel_id=1, source_target_pairs={{0,14},{1,15},{2,0},{3,1},{4,2},{5,3},{6,4},{7,5},{8,6},{9,7},{10,... | collective-permute-start | bytes 115208 | tf_op jit(solution)/shard_map/ppermute | solution.py:28
  381.0 62.9 %collective-permute-start.44 = (bf16[1,1,25,768]{3,2,1,0:T(8,128)(2,1)S(1)}, bf16[1,1,25,768]{3,2,1,0:T(8,128)(2,1)S(1)}, u32[]{:S(2)}, u32[]{:S(2)}) collective-permute-start(bf16[1,1,25,768]{3,2,1,0:T(8,128)(2,1)S(1)} %get-tuple-element.145), channel_id=1, source_target_pairs={{0,13},{1,14},{2,15},{3,0},{4,1},{5,2},{6,3},{7,4},{8,5},{9,6},{10... | collective-permute-start | bytes 115208 | tf_op jit(solution)/shard_map/ppermute | solution.py:28
  381.0 62.9 %collective-permute-start.43 = (bf16[1,1,25,768]{3,2,1,0:T(8,128)(2,1)S(1)}, bf16[1,1,25,768]{3,2,1,0:T(8,128)(2,1)S(1)}, u32[]{:S(2)}, u32[]{:S(2)}) collective-permute-start(bf16[1,1,25,768]{3,2,1,0:T(8,128)(2,1)S(1)} %get-tuple-element.146), channel_id=1, source_target_pairs={{0,12},{1,13},{2,14},{3,15},{4,0},{5,1},{6,2},{7,3},{8,4},{9,5},{1... | collective-permute-start | bytes 115208 | tf_op jit(solution)/shard_map/ppermute | solution.py:28
  503.5 67.6 %collective-permute-start.61 = (bf16[1,1,25,768]{3,2,1,0:T(8,128)(2,1)S(1)}, bf16[1,1,25,768]{3,2,1,0:T(8,128)(2,1)S(1)}, u32[]{:S(2)}, u32[]{:S(2)}) collective-permute-start(bf16[1,1,25,768]{3,2,1,0:T(8,128)(2,1)S(1)} %get-tuple-element.128), channel_id=1, source_target_pairs={{0,15},{1,0},{2,1},{3,2},{4,3},{5,4},{6,5},{7,6},{8,7},{9,8},{10,9... | collective-permute-start | bytes 115208 | tf_op jit(solution)/shard_map/ppermute | solution.py:28
  507.6 63.4 %collective-permute-start.60 = (bf16[1,1,25,768]{3,2,1,0:T(8,128)(2,1)S(1)}, bf16[1,1,25,768]{3,2,1,0:T(8,128)(2,1)S(1)}, u32[]{:S(2)}, u32[]{:S(2)}) collective-permute-start(bf16[1,1,25,768]{3,2,1,0:T(8,128)(2,1)S(1)} %get-tuple-element.129), channel_id=1, source_target_pairs={{0,14},{1,15},{2,0},{3,1},{4,2},{5,3},{6,4},{7,5},{8,6},{9,7},{10,... | collective-permute-start | bytes 115208 | tf_op jit(solution)/shard_map/ppermute | solution.py:28
  508.3 62.7 %collective-permute-start.59 = (bf16[1,1,25,768]{3,2,1,0:T(8,128)(2,1)S(1)}, bf16[1,1,25,768]{3,2,1,0:T(8,128)(2,1)S(1)}, u32[]{:S(2)}, u32[]{:S(2)}) collective-permute-start(bf16[1,1,25,768]{3,2,1,0:T(8,128)(2,1)S(1)} %get-tuple-element.130), channel_id=1, source_target_pairs={{0,13},{1,14},{2,15},{3,0},{4,1},{5,2},{6,3},{7,4},{8,5},{9,6},{10... | collective-permute-start | bytes 115208 | tf_op jit(solution)/shard_map/ppermute | solution.py:28
  508.3 62.7 %collective-permute-start.58 = (bf16[1,1,25,768]{3,2,1,0:T(8,128)(2,1)S(1)}, bf16[1,1,25,768]{3,2,1,0:T(8,128)(2,1)S(1)}, u32[]{:S(2)}, u32[]{:S(2)}) collective-permute-start(bf16[1,1,25,768]{3,2,1,0:T(8,128)(2,1)S(1)} %get-tuple-element.131), channel_id=1, source_target_pairs={{0,12},{1,13},{2,14},{3,15},{4,0},{5,1},{6,2},{7,3},{8,4},{9,5},{1... | collective-permute-start | bytes 115208 | tf_op jit(solution)/shard_map/ppermute | solution.py:28
  648.4 66.7 %collective-permute-start.77 = (bf16[1,1,25,768]{3,2,1,0:T(8,128)(2,1)S(1)}, bf16[1,1,25,768]{3,2,1,0:T(8,128)(2,1)S(1)}, u32[]{:S(2)}, u32[]{:S(2)}) collective-permute-start(bf16[1,1,25,768]{3,2,1,0:T(8,128)(2,1)S(1)} %get-tuple-element.113), channel_id=1, source_target_pairs={{0,15},{1,0},{2,1},{3,2},{4,3},{5,4},{6,5},{7,6},{8,7},{9,8},{10,9... | collective-permute-start | bytes 115208 | tf_op jit(solution)/shard_map/ppermute | solution.py:28
  652.5 62.5 %collective-permute-start.76 = (bf16[1,1,25,768]{3,2,1,0:T(8,128)(2,1)S(1)}, bf16[1,1,25,768]{3,2,1,0:T(8,128)(2,1)S(1)}, u32[]{:S(2)}, u32[]{:S(2)}) collective-permute-start(bf16[1,1,25,768]{3,2,1,0:T(8,128)(2,1)S(1)} %get-tuple-element.114), channel_id=1, source_target_pairs={{0,14},{1,15},{2,0},{3,1},{4,2},{5,3},{6,4},{7,5},{8,6},{9,7},{10,... | collective-permute-start | bytes 115208 | tf_op jit(solution)/shard_map/ppermute | solution.py:28
  653.2 61.8 %collective-permute-start.75 = (bf16[1,1,25,768]{3,2,1,0:T(8,128)(2,1)S(1)}, bf16[1,1,25,768]{3,2,1,0:T(8,128)(2,1)S(1)}, u32[]{:S(2)}, u32[]{:S(2)}) collective-permute-start(bf16[1,1,25,768]{3,2,1,0:T(8,128)(2,1)S(1)} %get-tuple-element.115), channel_id=1, source_target_pairs={{0,13},{1,14},{2,15},{3,0},{4,1},{5,2},{6,3},{7,4},{8,5},{9,6},{10... | collective-permute-start | bytes 115208 | tf_op jit(solution)/shard_map/ppermute | solution.py:28
  653.2 61.7 %collective-permute-start.74 = (bf16[1,1,25,768]{3,2,1,0:T(8,128)(2,1)S(1)}, bf16[1,1,25,768]{3,2,1,0:T(8,128)(2,1)S(1)}, u32[]{:S(2)}, u32[]{:S(2)}) collective-permute-start(bf16[1,1,25,768]{3,2,1,0:T(8,128)(2,1)S(1)} %get-tuple-element.116), channel_id=1, source_target_pairs={{0,12},{1,13},{2,14},{3,15},{4,0},{5,1},{6,2},{7,3},{8,4},{9,5},{1... | collective-permute-start | bytes 115208 | tf_op jit(solution)/shard_map/ppermute | solution.py:28
  795.9 67.3 %collective-permute-start.93 = (bf16[1,1,25,768]{3,2,1,0:T(8,128)(2,1)S(1)}, bf16[1,1,25,768]{3,2,1,0:T(8,128)(2,1)S(1)}, u32[]{:S(2)}, u32[]{:S(2)}) collective-permute-start(bf16[1,1,25,768]{3,2,1,0:T(8,128)(2,1)S(1)} %get-tuple-element.98), channel_id=1, source_target_pairs={{0,15},{1,0},{2,1},{3,2},{4,3},{5,4},{6,5},{7,6},{8,7},{9,8},{10,9... | collective-permute-start | bytes 115208 | tf_op jit(solution)/shard_map/ppermute | solution.py:28
  800.9 62.2 %collective-permute-start.92 = (bf16[1,1,25,768]{3,2,1,0:T(8,128)(2,1)S(1)}, bf16[1,1,25,768]{3,2,1,0:T(8,128)(2,1)S(1)}, u32[]{:S(2)}, u32[]{:S(2)}) collective-permute-start(bf16[1,1,25,768]{3,2,1,0:T(8,128)(2,1)S(1)} %get-tuple-element.99), channel_id=1, source_target_pairs={{0,14},{1,15},{2,0},{3,1},{4,2},{5,3},{6,4},{7,5},{8,6},{9,7},{10,... | collective-permute-start | bytes 115208 | tf_op jit(solution)/shard_map/ppermute | solution.py:28
  800.9 62.2 %collective-permute-start.91 = (bf16[1,1,25,768]{3,2,1,0:T(8,128)(2,1)S(1)}, bf16[1,1,25,768]{3,2,1,0:T(8,128)(2,1)S(1)}, u32[]{:S(2)}, u32[]{:S(2)}) collective-permute-start(bf16[1,1,25,768]{3,2,1,0:T(8,128)(2,1)S(1)} %get-tuple-element.100), channel_id=1, source_target_pairs={{0,13},{1,14},{2,15},{3,0},{4,1},{5,2},{6,3},{7,4},{8,5},{9,6},{10... | collective-permute-start | bytes 115208 | tf_op jit(solution)/shard_map/ppermute | solution.py:28
  800.9 62.2 %collective-permute-start.90 = (bf16[1,1,25,768]{3,2,1,0:T(8,128)(2,1)S(1)}, bf16[1,1,25,768]{3,2,1,0:T(8,128)(2,1)S(1)}, u32[]{:S(2)}, u32[]{:S(2)}) collective-permute-start(bf16[1,1,25,768]{3,2,1,0:T(8,128)(2,1)S(1)} %get-tuple-element.101), channel_id=1, source_target_pairs={{0,12},{1,13},{2,14},{3,15},{4,0},{5,1},{6,2},{7,3},{8,4},{9,5},{1... | collective-permute-start | bytes 115208 | tf_op jit(solution)/shard_map/ppermute | solution.py:28
  876.9 82.9 %reduce-scatter.8.cloned.1.call-start = ((), (), s32[]{:S(2)}) async-start(), calls=%async_computation.12 | async-start | bytes 1769472 | tf_op jit(solution)/shard_map/reduce_scatter | solution.py:369
  911.4 71.6 %reduce-scatter.6.cloned.1.call-start = ((), (), s32[]{:S(2)}) async-start(), calls=%async_computation.11 | async-start | bytes 5308416 | tf_op jit(solution)/shard_map/reduce_scatter | solution.py:369
  931.3 67.6 %reduce-scatter.10.cloned.1.call-start = ((), (), s32[]{:S(2)}) async-start(), calls=%async_computation.13 | async-start | bytes 294912
  951.7 157.2 %all-reduce.10.cloned.1.call-start = ((), (), s32[]{:S(2)}) async-start(), calls=%async_computation.14 | async-start | bytes 4718592 | tf_op jit(solution)/shard_map/psum | solution.py:372
  (228 other events, 3187.5 us)
Sparse Core Ops, SparseCore 0:
  9.5 52.1 all-gather.2
  63.2 22.7 all-gather.4
  911.5 20.9 reduce-scatter.7
  935.2 47.7 reduce-scatter.5
  985.0 11.0 reduce-scatter.9
  999.5 109.2 all-reduce.9
